TPU v7x, 32 devices: a whole 2x2x4 slice. The times are simulated.
32 devices in a mesh: groups: 2 (over x), probe: 16 (over z, y, core).
Axes of the slice: x: 2, y: 2, z: 4, core: 2. Of those that a mesh axis runs over, the one named last changes fastest.
Arguments:
- atom_positions: float32 [2, 32768], P(None, ('groups', 'probe')), parts along dimension 1, may hold values from 0 to 512
- atom_species: int32 [32768], P(('groups', 'probe')), parts along dimension 0, may hold values from 0 to 7
- atom_slice: int32 [32768], P(('groups', 'probe')), parts along dimension 0, may hold values from 0 to 3
- species_amp: float32 [8], replicated, may hold values from 0.02 to 0.125
- species_width: float32 [8], replicated, may hold values from 2 to 8
- probe_spectrum: float32 [2, 256, 256], replicated, may hold values from -6 to 6
- window_offsets: int32 [128, 2], P(('groups', 'probe')), parts along dimension 0, may hold values from 0 to 256
- probe_shifts: int32 [128, 2], P(('groups', 'probe')), parts along dimension 0, may hold values from 0 to 255
- slice_phase: float32 [3], replicated, may hold values from 0.0002746582 to 0.001373291
Outputs:
- scan_spectrum: float32 [2, 128, 65536], P(None, 'groups', 'probe'), parts along dimension 1
There are 2 independent parts, one for each index of `groups`. A program takes and returns all parts, laid end to end along the dimension named above; an argument that names none is the same for every part. Nothing has to cross between parts.
All inputs are finite; a program needn't handle non-finite values.
Results may differ from a plain program's by a relative error of at most 0.025.
Values may be sent and summed in bfloat16 or wider, within the bound.
No kernel may reach another device: no remote copies, remote signals or barrier semaphores. Data moves between devices by JAX's collectives and lax.ppermute only.
A program may use at most 64 MiB of HBM per device.

v0:
```python
import math
import jax
import jax.numpy as jnp
from jax import lax
from jax.sharding import PartitionSpec as P

G = 512
W = 256
SLICES = 4


def dft_tables(length):
    indices = jnp.arange(length, dtype=jnp.int32)
    angles = (
        2.0 * math.pi / length * (indices[:, None] * indices[None, :] % length).astype(jnp.float32)
    )
    factor = 1.0 / math.sqrt(length)
    return (
        (jnp.cos(angles) * factor).astype(jnp.bfloat16),
        (jnp.sin(angles) * factor).astype(jnp.bfloat16),
    )


def along_rows(real_part, imag_part, matrix, direction):
    batch_count = real_part.shape[0]
    length = real_part.shape[1]
    stacked = jnp.concatenate([real_part, imag_part], axis=0)
    product = jnp.einsum("ky,byx->bkx", matrix, stacked, preferred_element_type=jnp.float32)
    new_real = product[:batch_count, :length] - direction * product[batch_count:, length:]
    new_imag = product[batch_count:, :length] + direction * product[:batch_count, length:]
    return (new_real, new_imag)


def along_columns(real_part, imag_part, matrix, direction):
    batch_count = real_part.shape[0]
    length = real_part.shape[2]
    stacked = jnp.concatenate([real_part, imag_part], axis=0)
    product = jnp.einsum("byx,xl->byl", stacked, matrix, preferred_element_type=jnp.float32)
    new_real = product[:batch_count, :, :length] - direction * product[batch_count:, :, length:]
    new_imag = product[batch_count:, :, :length] + direction * product[:batch_count, :, length:]
    return (new_real, new_imag)


def transmit(real_part, imag_part, window):
    values = window.astype(jnp.float32)
    cosine = jnp.cos(values)
    sine = jnp.sin(values)
    return (
        (real_part * cosine - imag_part * sine).astype(jnp.bfloat16),
        (real_part * sine + imag_part * cosine).astype(jnp.bfloat16),
    )


def frequencies(length):
    indices = jnp.arange(length, dtype=jnp.int32)
    frequency = (indices + length // 2) % length - length // 2
    squared = frequency[:, None] * frequency[:, None] + frequency[None, :] * frequency[None, :]
    aperture = (9 * squared < length * length).astype(jnp.float32)
    return (squared.astype(jnp.float32), aperture)


def multislice(probe_spectrum, shifts, windows, slice_phase):
    length = probe_spectrum.shape[-1]
    cos_table, sin_table = dft_tables(length)
    rows_matrix = jnp.concatenate([cos_table, sin_table], axis=0)
    columns_matrix = jnp.concatenate([cos_table, sin_table], axis=1)
    squared, aperture = frequencies(length)
    indices = jnp.arange(length, dtype=jnp.int32)
    phase_index = (
        indices[None, :, None] * shifts[:, 0][:, None, None]
        + indices[None, None, :] * shifts[:, 1][:, None, None]
    ) % length
    angles = 2.0 * math.pi / length * phase_index.astype(jnp.float32)
    cosine = jnp.cos(angles)
    sine = jnp.sin(angles)
    real_part = (probe_spectrum[0] * cosine + probe_spectrum[1] * sine).astype(jnp.bfloat16)
    imag_part = (probe_spectrum[1] * cosine - probe_spectrum[0] * sine).astype(jnp.bfloat16)
    real_part, imag_part = along_rows(real_part, imag_part, rows_matrix, 1.0)
    real_part, imag_part = along_columns(
        real_part.astype(jnp.bfloat16), imag_part.astype(jnp.bfloat16), columns_matrix, 1.0
    )
    real_part, imag_part = transmit(real_part, imag_part, windows[0])
    for layer in range(len(windows) - 1):
        real_part, imag_part = along_rows(real_part, imag_part, rows_matrix, -1.0)
        real_part, imag_part = along_columns(
            real_part.astype(jnp.bfloat16), imag_part.astype(jnp.bfloat16), columns_matrix, -1.0
        )
        phases = slice_phase[layer] * squared
        prop_real = aperture * jnp.cos(phases)
        prop_imag = -aperture * jnp.sin(phases)
        new_real = (real_part * prop_real - imag_part * prop_imag).astype(jnp.bfloat16)
        new_imag = (real_part * prop_imag + imag_part * prop_real).astype(jnp.bfloat16)
        real_part, imag_part = along_rows(new_real, new_imag, rows_matrix, 1.0)
        real_part, imag_part = along_columns(
            real_part.astype(jnp.bfloat16), imag_part.astype(jnp.bfloat16), columns_matrix, 1.0
        )
        real_part, imag_part = transmit(real_part, imag_part, windows[layer + 1])
    real_part, imag_part = along_rows(real_part, imag_part, rows_matrix, -1.0)
    real_part, imag_part = along_columns(
        real_part.astype(jnp.bfloat16), imag_part.astype(jnp.bfloat16), columns_matrix, -1.0
    )
    return (aperture * (real_part * real_part + imag_part * imag_part)).astype(jnp.bfloat16)


def atom_factors(
    atom_positions, atom_species, atom_slice, species_amp, species_width, grid, layers
):
    species_ids = jnp.arange(species_amp.shape[0], dtype=jnp.int32)
    selector = (atom_species[:, None] == species_ids[None, :]).astype(jnp.float32)
    amplitude = jnp.sum(selector * species_amp[None, :], axis=1)
    widths = jnp.sum(selector * species_width[None, :], axis=1)
    inverse_spread = 0.5 / (widths * widths)
    pixels = jnp.arange(grid, dtype=jnp.float32)
    along_y = jnp.exp(
        -jnp.square(pixels[:, None] - atom_positions[0][None, :]) * inverse_spread[None, :]
    )
    layer_ids = jnp.arange(layers, dtype=jnp.int32)
    weight = amplitude[None, :] * (atom_slice[None, :] == layer_ids[:, None]).astype(jnp.float32)
    row_factor = (
        (weight[:, None, :] * along_y[None, :, :]).astype(jnp.bfloat16).reshape(layers * grid, -1)
    )
    column_factor = jnp.exp(
        -jnp.square(pixels[None, :] - atom_positions[1][:, None]) * inverse_spread[:, None]
    ).astype(jnp.bfloat16)
    return (row_factor, column_factor)


def scan_transform(received):
    intensity = received[:, 0, :]
    positions = intensity.shape[0]
    cos_scan, sin_scan = dft_tables(positions)
    matrix = jnp.concatenate([cos_scan, sin_scan], axis=0)
    product = jnp.dot(matrix, intensity, preferred_element_type=jnp.float32)
    return jnp.stack([product[:positions], -product[positions:]], axis=0)


def on_device(
    atom_positions,
    atom_species,
    atom_slice,
    species_amp,
    species_width,
    probe_spectrum,
    window_offsets,
    probe_shifts,
    slice_phase,
):
    devices = lax.axis_size("probe")
    row_factor, column_factor = atom_factors(
        atom_positions, atom_species, atom_slice, species_amp, species_width, G, SLICES
    )
    partial_field = jnp.dot(row_factor, column_factor, preferred_element_type=jnp.float32)
    whole_field = lax.psum(partial_field, "probe").astype(jnp.bfloat16).reshape(SLICES, G, G)
    slabs = [whole_field[layer] for layer in range(SLICES)]
    windows = []
    for slab in slabs:
        windows.append(
            jax.vmap(lambda corner: lax.dynamic_slice(slab, (corner[0], corner[1]), (W, W)))(
                window_offsets
            )
        )
    intensity = multislice(probe_spectrum, probe_shifts, windows, slice_phase)
    local_count = intensity.shape[0]
    pieces = intensity.reshape(local_count, devices, W * W // devices)
    return scan_transform(lax.all_to_all(pieces, "probe", split_axis=1, concat_axis=0, tiled=True))


def solution(mesh):
    placed = (
        P(None, ("groups", "probe")),
        P(("groups", "probe")),
        P(("groups", "probe")),
        P(),
        P(),
        P(),
        P(("groups", "probe"), None),
        P(("groups", "probe"), None),
        P(),
    )
    return jax.shard_map(
        on_device, mesh=mesh, in_specs=placed, out_specs=P(None, "groups", "probe"), check_vma=False
    )
```

profile of v0, /device:TPU:0, one launch (start us, length us, event | category | flops | bytes accessed | tf_op | source)
XLA Modules:
  0.0 217.3 jit_solution(16012172392962101634)
XLA Ops:
  0.0 1.1 multiply_convert_fusion.1
  1.1 0.8 select_reduce_fusion.1
  1.9 0.8 fusion.193
  3.2 0.7 fusion.167
  3.9 1.1 multiply_convert_fusion
  5.0 4.6 %fusion.16 = f32[2048,512]{1,0:T(8,128)} fusion(bf16[2048,1024]{1,0:T(8,128)(2,1)S(1)} %bitcast.101, f32[1024]{0:T(1024)S(1)} %multiply_divide_fusion, f32[1024]{0:T(1024)S(1)} %bitcast.104), kind=kOutput, calls=%fused_computation.49 | convolution fusion | flops 2150105088 | bytes 8396800 | tf_op jit(solution)/shard_map/dot_general | solution.py:152
  9.5 97.1 %all-reduce.1 = bf16[2048,512]{1,0:T(8,128)(2,1)S(1)} all-reduce(f32[2048,512]{1,0:T(8,128)} %fusion.16), channel_id=1, replica_groups=mesh['groups'=2,'probe'=16] {'probe'}, use_global_device_ids=true, to_apply=%region_2.0 | all-reduce | flops 1048576 | bytes 6291456 | tf_op jit(solution)/shard_map/psum | solution.py:153
  106.6 1.2 fusion.192
  107.8 11.6 %while.7 = (s32[]{:T(128)}, bf16[512,512]{1,0:T(8,128)(2,1)}, s32[4,2]{0,1:T(2,128)S(1)}, bf16[4,256,256]{2,1,0:T(8,128)(2,1)S(1)}, s32[]{:T(128)}) while((s32[]{:T(128)}, bf16[512,512]{1,0:T(8,128)(2,1)}, s32[4,2]{0,1:T(2,128)S(1)}, bf16[4,256,256]{2,1,0:T(8,128)(2,1)S(1)}, s32[]{:T(128)}) %tuple.96), condition=%wide.while_cond.3, body=%wide.while_body.3.sunk | while | flops 2 | bytes 262261 | solution.py:158
  107.9 0.5 fusion.204
  108.5 2.2 %bitcast_dynamic-update-slice_fusion.11 = bf16[4,256,256]{2,1,0:T(8,128)(2,1)S(1)} fusion(bf16[4,256,256]{2,1,0:T(8,128)(2,1)S(1)} %get-tuple-element.264, s32[]{:T(128)S(6)} %copy.159, bf16[512,512]{1,0:T(8,128)(2,1)} %get-tuple-element.267, s32[]{:T(128)} %bitcast.99, s32[]{:T(128)} %bitcast.100), kind=kLoop, calls=%fused_computation.6.clone.1 | loop fusion | bytes 262156 | tf_op jit(solution)/shard_map/vmap()/gather
  110.8 0.5 fusion.204
  111.4 2.2 %bitcast_dynamic-update-slice_fusion.11 = bf16[4,256,256]{2,1,0:T(8,128)(2,1)S(1)} fusion(bf16[4,256,256]{2,1,0:T(8,128)(2,1)S(1)} %get-tuple-element.264, s32[]{:T(128)S(6)} %copy.159, bf16[512,512]{1,0:T(8,128)(2,1)} %get-tuple-element.267, s32[]{:T(128)} %bitcast.99, s32[]{:T(128)} %bitcast.100), kind=kLoop, calls=%fused_computation.6.clone.1 | loop fusion | bytes 262156 | tf_op jit(solution)/shard_map/vmap()/gather
  113.7 0.5 fusion.204
  114.3 2.2 %bitcast_dynamic-update-slice_fusion.11 = bf16[4,256,256]{2,1,0:T(8,128)(2,1)S(1)} fusion(bf16[4,256,256]{2,1,0:T(8,128)(2,1)S(1)} %get-tuple-element.264, s32[]{:T(128)S(6)} %copy.159, bf16[512,512]{1,0:T(8,128)(2,1)} %get-tuple-element.267, s32[]{:T(128)} %bitcast.99, s32[]{:T(128)} %bitcast.100), kind=kLoop, calls=%fused_computation.6.clone.1 | loop fusion | bytes 262156 | tf_op jit(solution)/shard_map/vmap()/gather
  116.6 0.5 fusion.204
  117.1 2.2 %bitcast_dynamic-update-slice_fusion.11 = bf16[4,256,256]{2,1,0:T(8,128)(2,1)S(1)} fusion(bf16[4,256,256]{2,1,0:T(8,128)(2,1)S(1)} %get-tuple-element.264, s32[]{:T(128)S(6)} %copy.159, bf16[512,512]{1,0:T(8,128)(2,1)} %get-tuple-element.267, s32[]{:T(128)} %bitcast.99, s32[]{:T(128)} %bitcast.100), kind=kLoop, calls=%fused_computation.6.clone.1 | loop fusion | bytes 262156 | tf_op jit(solution)/shard_map/vmap()/gather
  119.4 0.7 fusion.194
  120.1 11.9 %while.6 = (s32[]{:T(128)}, bf16[512,512]{1,0:T(8,128)(2,1)}, s32[4,2]{0,1:T(2,128)S(1)}, bf16[4,256,256]{2,1,0:T(8,128)(2,1)S(1)}, s32[]{:T(128)}) while((s32[]{:T(128)}, bf16[512,512]{1,0:T(8,128)(2,1)}, s32[4,2]{0,1:T(2,128)S(1)}, bf16[4,256,256]{2,1,0:T(8,128)(2,1)S(1)}, s32[]{:T(128)}) %tuple.108), condition=%wide.while_cond.2, body=%wide.while_body.2.sunk | while | flops 2 | bytes 262261 | solution.py:158
  120.2 0.6 fusion.203
  120.8 2.3 %bitcast_dynamic-update-slice_fusion.10 = bf16[4,256,256]{2,1,0:T(8,128)(2,1)S(1)} fusion(bf16[4,256,256]{2,1,0:T(8,128)(2,1)S(1)} %get-tuple-element.279, s32[]{:T(128)S(6)} %copy.165, bf16[512,512]{1,0:T(8,128)(2,1)} %get-tuple-element.282, s32[]{:T(128)} %bitcast.96, s32[]{:T(128)} %bitcast.97), kind=kLoop, calls=%fused_computation.4.clone.1 | loop fusion | bytes 262156 | tf_op jit(solution)/shard_map/vmap()/gather
  123.2 0.6 fusion.203
  123.8 2.3 %bitcast_dynamic-update-slice_fusion.10 = bf16[4,256,256]{2,1,0:T(8,128)(2,1)S(1)} fusion(bf16[4,256,256]{2,1,0:T(8,128)(2,1)S(1)} %get-tuple-element.279, s32[]{:T(128)S(6)} %copy.165, bf16[512,512]{1,0:T(8,128)(2,1)} %get-tuple-element.282, s32[]{:T(128)} %bitcast.96, s32[]{:T(128)} %bitcast.97), kind=kLoop, calls=%fused_computation.4.clone.1 | loop fusion | bytes 262156 | tf_op jit(solution)/shard_map/vmap()/gather
  126.1 0.6 fusion.203
  126.7 2.3 %bitcast_dynamic-update-slice_fusion.10 = bf16[4,256,256]{2,1,0:T(8,128)(2,1)S(1)} fusion(bf16[4,256,256]{2,1,0:T(8,128)(2,1)S(1)} %get-tuple-element.279, s32[]{:T(128)S(6)} %copy.165, bf16[512,512]{1,0:T(8,128)(2,1)} %get-tuple-element.282, s32[]{:T(128)} %bitcast.96, s32[]{:T(128)} %bitcast.97), kind=kLoop, calls=%fused_computation.4.clone.1 | loop fusion | bytes 262156 | tf_op jit(solution)/shard_map/vmap()/gather
  129.1 0.6 fusion.203
  129.7 2.3 %bitcast_dynamic-update-slice_fusion.10 = bf16[4,256,256]{2,1,0:T(8,128)(2,1)S(1)} fusion(bf16[4,256,256]{2,1,0:T(8,128)(2,1)S(1)} %get-tuple-element.279, s32[]{:T(128)S(6)} %copy.165, bf16[512,512]{1,0:T(8,128)(2,1)} %get-tuple-element.282, s32[]{:T(128)} %bitcast.96, s32[]{:T(128)} %bitcast.97), kind=kLoop, calls=%fused_computation.4.clone.1 | loop fusion | bytes 262156 | tf_op jit(solution)/shard_map/vmap()/gather
  132.0 7.8 %while.5 = (s32[]{:T(128)}, bf16[512,512]{1,0:T(8,128)(2,1)S(1)}, s32[4,2]{0,1:T(2,128)S(1)}, bf16[4,256,256]{2,1,0:T(8,128)(2,1)S(1)}, s32[]{:T(128)}) while((s32[]{:T(128)}, bf16[512,512]{1,0:T(8,128)(2,1)S(1)}, s32[4,2]{0,1:T(2,128)S(1)}, bf16[4,256,256]{2,1,0:T(8,128)(2,1)S(1)}, s32[]{:T(128)}) %tuple.109), condition=%wide.while_cond.1, body=%wide.while_body.1.sunk | while | flops 2 | bytes 262261 | solution.py:158
  132.6 1.3 bitcast_dynamic-update-slice_fusion.9
  134.6 1.3 bitcast_dynamic-update-slice_fusion.9
  136.5 1.3 bitcast_dynamic-update-slice_fusion.9
  138.5 1.3 bitcast_dynamic-update-slice_fusion.9
  139.9 7.8 %while.4 = (s32[]{:T(128)}, bf16[512,512]{1,0:T(8,128)(2,1)S(1)}, s32[4,2]{0,1:T(2,128)S(1)}, bf16[4,256,256]{2,1,0:T(8,128)(2,1)S(1)}, s32[]{:T(128)}) while((s32[]{:T(128)}, bf16[512,512]{1,0:T(8,128)(2,1)S(1)}, s32[4,2]{0,1:T(2,128)S(1)}, bf16[4,256,256]{2,1,0:T(8,128)(2,1)S(1)}, s32[]{:T(128)}) %tuple.110), condition=%wide.while_cond, body=%wide.while_body.sunk | while | flops 2 | bytes 262261 | solution.py:158
  140.5 1.3 bitcast_dynamic-update-slice_fusion.8
  142.4 1.3 bitcast_dynamic-update-slice_fusion.8
  144.4 1.3 bitcast_dynamic-update-slice_fusion.8
  146.3 1.3 bitcast_dynamic-update-slice_fusion.8
  147.7 1.1 slice_bitcast_fusion.2
  149.1 4.8 %add_convert_fusion.3 = (bf16[4,256,256]{1,2,0:T(8,128)(2,1)S(1)}, bf16[4,256,256]{1,2,0:T(8,128)(2,1)S(1)}) fusion(f32[256,256]{0,1:T(8,128)S(1)} %copy.105, s32[4,256]{1,0:T(4,128)S(1)} %get-tuple-element.134, s32[4,256]{1,0:T(4,128)S(1)} %get-tuple-element.135, f32[256,256]{0,1:T(8,128)S(1)} %copy.104), kind=kLoop, calls=%fused_computation.206 | loop fusion | flops 5767168 | bytes 1581056 | tf_op jit(solution)/shard_map/convert_element_type | solution.py:76
  153.9 0.7 convolution_bitcast_fusion.7
  154.9 0.8 fusion.77
  155.7 4.1 %fusion.30 = (bf16[4,256,256]{2,1,0:T(8,128)(2,1)S(1)}, bf16[4,256,256]{2,1,0:T(8,128)(2,1)S(1)}) fusion(bf16[4,256,256]{2,1,0:T(8,128)(2,1)S(1)} %get-tuple-element.12, f32[8,256,512]{2,1,0:T(8,128)S(1)} %fusion.77), kind=kLoop, calls=%fused_computation.63 | loop fusion | flops 2883584 | bytes 5767168 | tf_op jit(solution)/shard_map/convert_element_type | solution.py:49
  159.8 0.8 convolution_bitcast_fusion.6
  161.1 0.8 fusion.84
  161.8 4.7 %fusion.147 = (f32[256,256]{0,1:T(8,128)S(1)}, f32[256,256]{0,1:T(8,128)S(1)}, f32[256,256]{0,1:T(8,128)S(1)}, f32[256,256]{0,1:T(8,128)S(1)}, f32[256,256]{0,1:T(8,128)S(1)}, /*index=5*/f32[256,256]{0,1:T(8,128)S(1)}) fusion(f32[]{:T(128)} %bitcast.11, s32[256]{0:T(256)S(1)} %fusion.169, f32[]{:T(128)} %bitcast.17, f32[]{:T(128)} %bitcast.14), kind=kLoop, calls=%fused_computation.227 | loop fusion | flops 983040 | bytes 1573900 | tf_op jit(solution)/shard_map/mul | solution.py:89
  167.0 0.7 convolution_bitcast_fusion.5
  168.1 0.8 fusion.91
  168.8 4.3 %fusion.26 = (bf16[4,256,256]{2,1,0:T(8,128)(2,1)S(1)}, bf16[4,256,256]{2,1,0:T(8,128)(2,1)S(1)}) fusion(bf16[4,256,256]{2,1,0:T(8,128)(2,1)S(1)} %get-tuple-element.20, f32[8,256,512]{2,1,0:T(8,128)S(1)} %fusion.91), kind=kLoop, calls=%fused_computation.59 | loop fusion | flops 2883584 | bytes 5767168 | tf_op jit(solution)/shard_map/convert_element_type | solution.py:49
  173.2 0.8 convolution_bitcast_fusion.4
  174.3 0.8 fusion.98
  175.6 0.7 convolution_bitcast_fusion.3
  176.6 0.8 fusion.105
  177.4 4.1 %fusion.22 = (bf16[4,256,256]{2,1,0:T(8,128)(2,1)S(1)}, bf16[4,256,256]{2,1,0:T(8,128)(2,1)S(1)}) fusion(bf16[4,256,256]{2,1,0:T(8,128)(2,1)S(1)} %get-tuple-element.28, f32[8,256,512]{2,1,0:T(8,128)S(1)} %fusion.105), kind=kLoop, calls=%fused_computation.55 | loop fusion | flops 2883584 | bytes 5767168 | tf_op jit(solution)/shard_map/convert_element_type | solution.py:49
  181.5 0.8 convolution_bitcast_fusion.2
  182.6 0.8 fusion.112
  183.9 0.7 convolution_bitcast_fusion.1
  184.9 0.8 fusion.119
  185.7 4.4 %fusion.18 = (bf16[4,256,256]{2,1,0:T(8,128)(2,1)S(1)}, bf16[4,256,256]{2,1,0:T(8,128)(2,1)S(1)}) fusion(bf16[4,256,256]{2,1,0:T(8,128)(2,1)S(1)} %get-tuple-element.36, f32[8,256,512]{2,1,0:T(8,128)S(1)} %fusion.119), kind=kLoop, calls=%fused_computation.51 | loop fusion | flops 2883584 | bytes 5767168 | tf_op jit(solution)/shard_map/convert_element_type | solution.py:49
  190.1 0.8 convolution_bitcast_fusion
  191.2 0.8 fusion.126
  192.9 1.2 copy.135
  194.1 6.8 %all-to-all-start = ((bf16[4,16,4096]{2,0,1:T(4,128)(2,1)}), bf16[4,16,4096]{2,0,1:T(4,128)(2,1)S(1)}, u32[]{:S(2)}, u32[]{:S(2)}) async-start(bf16[4,16,4096]{2,0,1:T(4,128)(2,1)} %copy.135), calls=%async_computation | async-start | bytes 1048576 | tf_op jit(solution)/shard_map/all_to_all | solution.py:165
  201.0 14.1 %all-to-all-done = bf16[4,16,4096]{2,0,1:T(4,128)(2,1)S(1)} async-done(((bf16[4,16,4096]{2,0,1:T(4,128)(2,1)}), bf16[4,16,4096]{2,0,1:T(4,128)(2,1)S(1)}, u32[]{:S(2)}, u32[]{:S(2)}) %all-to-all-start) | async-done | bytes 524320 | tf_op jit(solution)/shard_map/all_to_all | solution.py:165
  215.9 1.5 pad_maximum_fusion
  (62 shorter events, 12.1 us)
Async XLA Ops:
  9.5 98.3 %copy-start.1 = (s32[4,2]{0,1:T(2,128)S(1)}, s32[4,2]{0,1:T(2,128)}, u32[]{:S(2)}) copy-start(s32[4,2]{0,1:T(2,128)} %param.15) | copy-start | bytes 100
  106.6 12.8 %copy-start = (f32[3]{0:T(128)S(1)}, f32[3]{0:T(128)}, u32[]{:S(2)}) copy-start(f32[3]{0:T(128)} %param.17) | copy-start | bytes 40
  119.4 29.5 %copy-start.2 = (s32[4,2]{0,1:T(2,128)S(1)}, s32[4,2]{0,1:T(2,128)}, u32[]{:S(2)}) copy-start(s32[4,2]{0,1:T(2,128)} %param.16) | copy-start | bytes 100
  194.1 21.1 %all-to-all-start = ((bf16[4,16,4096]{2,0,1:T(4,128)(2,1)}), bf16[4,16,4096]{2,0,1:T(4,128)(2,1)S(1)}, u32[]{:S(2)}, u32[]{:S(2)}) async-start(bf16[4,16,4096]{2,0,1:T(4,128)(2,1)} %copy.135), calls=%async_computation | async-start | bytes 1048576 | tf_op jit(solution)/shard_map/all_to_all | solution.py:165
where the time goes:
time: 218 us; the launch traced here: 217 us
  blocking collectives  97.1 us (45%)
  local copies, waits for them, and re-layouts  44.5 us (20%)
  other arithmetic  36.9 us (17%)
  matrix products  17.2 us (8%)
  waiting for transfers between devices  14.1 us (6%)
  starting transfers between devices  6.8 us (3%)
    psum x1, blocking collectives, on_device(): lax.psum(partial_field, 'probe').astype(jnp.bfloat16).reshape(SLICES, G, G)  97.1 us
    gather x48, local copies, waits for them, and re-layouts  38.6 us
    convert_element_type x4, other arithmetic, transmit(): (real_part * cosine - imag_part * sine).astype(jnp.bfloat16)  17 us
    all_to_all x1, waiting for transfers between devices, on_device(): lax.all_to_all(pieces, 'probe', split_axis=1, concat_axis=0, tiled=True)  14.1 us
    all_to_all x1, starting transfers between devices, on_device(): lax.all_to_all(pieces, 'probe', split_axis=1, concat_axis=0, tiled=True)  6.8 us
    dot_general x8, matrix products, along_columns(): jnp.einsum('byx,xl->byl', stacked, matrix, preferred_element_type=jnp.flo...  6.17 us
    dot_general x8, matrix products, along_rows(): jnp.einsum('ky,byx->bkx', matrix, stacked, preferred_element_type=jnp.flo...  6.03 us
    convert_element_type x1, other arithmetic, multislice(): (probe_spectrum[0] * cosine + probe_spectrum[1] * sine).astype(jnp.bfloat16)  4.77 us
  transfers between devices with their start and end apart: 1, of which 1 were waited for; matrix products, arithmetic and copies ran while one was open for 0% of the time, Pallas kernels for 0%

commit v1 on v0

--- a/solution.py
+++ b/solution.py
@@ -7,6 +7,13 @@
 G = 512
 W = 256
 SLICES = 4
+
+
+def swap_blocks(x, axis, split, join):
+    peers = lax.axis_size(axis)
+    shards = jnp.stack(jnp.split(x, peers, axis=split), axis=0)
+    shards = lax.all_to_all(shards, axis, split_axis=0, concat_axis=0)
+    return jnp.concatenate(shards, axis=join)
 
 
 def dft_tables(length):
@@ -162,7 +169,7 @@
     intensity = multislice(probe_spectrum, probe_shifts, windows, slice_phase)
     local_count = intensity.shape[0]
     pieces = intensity.reshape(local_count, devices, W * W // devices)
-    return scan_transform(lax.all_to_all(pieces, "probe", split_axis=1, concat_axis=0, tiled=True))
+    return scan_transform(swap_blocks(pieces, "probe", 1, 0))
 
 
 def solution(mesh):

time: 218 us -> 231 us (1.060)
  local copies, waits for them, and re-layouts: 44.5 us -> 57.1 us
    unnamed x10 -> x25, local copies, waits for them, and re-layouts: 0.17 us -> 10.1 us
    gather x48, local copies, waits for them, and re-layouts: 38.6 us -> 41 us
where the time goes in v1:
time: 231 us; the launch traced here: 230 us
  blocking collectives  97.1 us (42%)
  local copies, waits for them, and re-layouts  57.1 us (25%)
  other arithmetic  36.9 us (16%)
  matrix products  17.2 us (7%)
  waiting for transfers between devices  14.1 us (6%)
  starting transfers between devices  6.8 us (3%)
    psum x1, blocking collectives, on_device(): lax.psum(partial_field, 'probe').astype(jnp.bfloat16).reshape(SLICES, G, G)  97.1 us
    gather x48, local copies, waits for them, and re-layouts  41 us
    convert_element_type x4, other arithmetic, transmit(): (real_part * cosine - imag_part * sine).astype(jnp.bfloat16)  17 us
    all_to_all x1, waiting for transfers between devices, swap_blocks(): shards = lax.all_to_all(shards, axis, split_axis=0, concat_axis=0)  14.1 us
    unnamed x25, local copies, waits for them, and re-layouts  10.1 us
    all_to_all x1, starting transfers between devices, swap_blocks(): shards = lax.all_to_all(shards, axis, split_axis=0, concat_axis=0)  6.8 us
    dot_general x8, matrix products, along_columns(): jnp.einsum('byx,xl->byl', stacked, matrix, preferred_element_type=jnp.flo...  6.17 us
    dot_general x8, matrix products, along_rows(): jnp.einsum('ky,byx->bkx', matrix, stacked, preferred_element_type=jnp.flo...  6.03 us
  transfers between devices with their start and end apart: 1, of which 1 were waited for; matrix products, arithmetic and copies ran while one was open for 0% of the time, Pallas kernels for 0%

profile of v1, /device:TPU:0, one launch (start us, length us, event | category | flops | bytes accessed | tf_op | source)
XLA Modules:
  0.0 230.0 jit_solution(14536529735462952546)
XLA Ops:
  0.0 1.1 multiply_convert_fusion.1
  1.1 0.8 select_reduce_fusion.1
  1.9 0.8 fusion.194
  3.2 0.7 fusion.167
  3.9 1.1 multiply_convert_fusion
  5.0 4.5 %fusion.16 = f32[2048,512]{1,0:T(8,128)} fusion(bf16[2048,1024]{1,0:T(8,128)(2,1)S(1)} %bitcast.130, f32[1024]{0:T(1024)S(1)} %multiply_divide_fusion, f32[1024]{0:T(1024)S(1)} %bitcast.132), kind=kOutput, calls=%fused_computation.49 | convolution fusion | flops 2150105088 | bytes 8396800 | tf_op jit(solution)/shard_map/dot_general | solution.py:159
  9.5 97.1 %all-reduce.1 = bf16[2048,512]{1,0:T(8,128)(2,1)S(1)} all-reduce(f32[2048,512]{1,0:T(8,128)} %fusion.16), channel_id=1, replica_groups=mesh['groups'=2,'probe'=16] {'probe'}, use_global_device_ids=true, to_apply=%region_2.0 | all-reduce | flops 1048576 | bytes 6291456 | tf_op jit(solution)/shard_map/psum | solution.py:160
  106.6 1.2 fusion.192
  107.8 12.0 %while.7 = (s32[]{:T(128)}, bf16[512,512]{1,0:T(8,128)(2,1)}, s32[4,2]{0,1:T(2,128)S(1)}, bf16[4,256,256]{2,1,0:T(8,128)(2,1)S(1)}, s32[]{:T(128)}) while((s32[]{:T(128)}, bf16[512,512]{1,0:T(8,128)(2,1)}, s32[4,2]{0,1:T(2,128)S(1)}, bf16[4,256,256]{2,1,0:T(8,128)(2,1)S(1)}, s32[]{:T(128)}) %tuple.111), condition=%wide.while_cond.3, body=%wide.while_body.3.sunk | while | flops 2 | bytes 262261 | solution.py:165
  108.5 2.3 %bitcast_dynamic-update-slice_fusion.11 = bf16[4,256,256]{2,1,0:T(8,128)(2,1)S(1)} fusion(bf16[4,256,256]{2,1,0:T(8,128)(2,1)S(1)} %get-tuple-element.280, s32[]{:T(128)S(6)} %copy.742, bf16[512,512]{1,0:T(8,128)(2,1)} %get-tuple-element.283, s32[]{:T(128)} %bitcast.128, s32[]{:T(128)} %bitcast.129), kind=kLoop, calls=%fused_computation.6.clone.1 | loop fusion | bytes 262156 | tf_op jit(solution)/shard_map/vmap()/gather
  111.5 2.3 %bitcast_dynamic-update-slice_fusion.11 = bf16[4,256,256]{2,1,0:T(8,128)(2,1)S(1)} fusion(bf16[4,256,256]{2,1,0:T(8,128)(2,1)S(1)} %get-tuple-element.280, s32[]{:T(128)S(6)} %copy.742, bf16[512,512]{1,0:T(8,128)(2,1)} %get-tuple-element.283, s32[]{:T(128)} %bitcast.128, s32[]{:T(128)} %bitcast.129), kind=kLoop, calls=%fused_computation.6.clone.1 | loop fusion | bytes 262156 | tf_op jit(solution)/shard_map/vmap()/gather
  114.5 2.3 %bitcast_dynamic-update-slice_fusion.11 = bf16[4,256,256]{2,1,0:T(8,128)(2,1)S(1)} fusion(bf16[4,256,256]{2,1,0:T(8,128)(2,1)S(1)} %get-tuple-element.280, s32[]{:T(128)S(6)} %copy.742, bf16[512,512]{1,0:T(8,128)(2,1)} %get-tuple-element.283, s32[]{:T(128)} %bitcast.128, s32[]{:T(128)} %bitcast.129), kind=kLoop, calls=%fused_computation.6.clone.1 | loop fusion | bytes 262156 | tf_op jit(solution)/shard_map/vmap()/gather
  117.5 2.3 %bitcast_dynamic-update-slice_fusion.11 = bf16[4,256,256]{2,1,0:T(8,128)(2,1)S(1)} fusion(bf16[4,256,256]{2,1,0:T(8,128)(2,1)S(1)} %get-tuple-element.280, s32[]{:T(128)S(6)} %copy.742, bf16[512,512]{1,0:T(8,128)(2,1)} %get-tuple-element.283, s32[]{:T(128)} %bitcast.128, s32[]{:T(128)} %bitcast.129), kind=kLoop, calls=%fused_computation.6.clone.1 | loop fusion | bytes 262156 | tf_op jit(solution)/shard_map/vmap()/gather
  120.5 12.4 %while.6 = (s32[]{:T(128)}, bf16[512,512]{1,0:T(8,128)(2,1)}, s32[4,2]{0,1:T(2,128)S(1)}, bf16[4,256,256]{2,1,0:T(8,128)(2,1)S(1)}, s32[]{:T(128)}) while((s32[]{:T(128)}, bf16[512,512]{1,0:T(8,128)(2,1)}, s32[4,2]{0,1:T(2,128)S(1)}, bf16[4,256,256]{2,1,0:T(8,128)(2,1)S(1)}, s32[]{:T(128)}) %tuple.123), condition=%wide.while_cond.2, body=%wide.while_body.2.sunk | while | flops 2 | bytes 262261 | solution.py:165
  121.2 2.4 %bitcast_dynamic-update-slice_fusion.10 = bf16[4,256,256]{2,1,0:T(8,128)(2,1)S(1)} fusion(bf16[4,256,256]{2,1,0:T(8,128)(2,1)S(1)} %get-tuple-element.295, s32[]{:T(128)S(6)} %copy.748, bf16[512,512]{1,0:T(8,128)(2,1)} %get-tuple-element.298, s32[]{:T(128)} %bitcast.125, s32[]{:T(128)} %bitcast.126), kind=kLoop, calls=%fused_computation.4.clone.1 | loop fusion | bytes 262156 | tf_op jit(solution)/shard_map/vmap()/gather
  124.3 2.4 %bitcast_dynamic-update-slice_fusion.10 = bf16[4,256,256]{2,1,0:T(8,128)(2,1)S(1)} fusion(bf16[4,256,256]{2,1,0:T(8,128)(2,1)S(1)} %get-tuple-element.295, s32[]{:T(128)S(6)} %copy.748, bf16[512,512]{1,0:T(8,128)(2,1)} %get-tuple-element.298, s32[]{:T(128)} %bitcast.125, s32[]{:T(128)} %bitcast.126), kind=kLoop, calls=%fused_computation.4.clone.1 | loop fusion | bytes 262156 | tf_op jit(solution)/shard_map/vmap()/gather
  127.3 2.4 %bitcast_dynamic-update-slice_fusion.10 = bf16[4,256,256]{2,1,0:T(8,128)(2,1)S(1)} fusion(bf16[4,256,256]{2,1,0:T(8,128)(2,1)S(1)} %get-tuple-element.295, s32[]{:T(128)S(6)} %copy.748, bf16[512,512]{1,0:T(8,128)(2,1)} %get-tuple-element.298, s32[]{:T(128)} %bitcast.125, s32[]{:T(128)} %bitcast.126), kind=kLoop, calls=%fused_computation.4.clone.1 | loop fusion | bytes 262156 | tf_op jit(solution)/shard_map/vmap()/gather
  130.4 2.4 %bitcast_dynamic-update-slice_fusion.10 = bf16[4,256,256]{2,1,0:T(8,128)(2,1)S(1)} fusion(bf16[4,256,256]{2,1,0:T(8,128)(2,1)S(1)} %get-tuple-element.295, s32[]{:T(128)S(6)} %copy.748, bf16[512,512]{1,0:T(8,128)(2,1)} %get-tuple-element.298, s32[]{:T(128)} %bitcast.125, s32[]{:T(128)} %bitcast.126), kind=kLoop, calls=%fused_computation.4.clone.1 | loop fusion | bytes 262156 | tf_op jit(solution)/shard_map/vmap()/gather
  132.9 8.5 %while.5 = (s32[]{:T(128)}, bf16[512,512]{1,0:T(8,128)(2,1)S(1)}, s32[4,2]{0,1:T(2,128)S(1)}, bf16[4,256,256]{2,1,0:T(8,128)(2,1)S(1)}, s32[]{:T(128)}) while((s32[]{:T(128)}, bf16[512,512]{1,0:T(8,128)(2,1)S(1)}, s32[4,2]{0,1:T(2,128)S(1)}, bf16[4,256,256]{2,1,0:T(8,128)(2,1)S(1)}, s32[]{:T(128)}) %tuple.124), condition=%wide.while_cond.1, body=%wide.while_body.1.sunk | while | flops 2 | bytes 262261 | solution.py:165
  133.6 1.4 bitcast_dynamic-update-slice_fusion.9
  135.7 1.4 bitcast_dynamic-update-slice_fusion.9
  137.8 1.4 bitcast_dynamic-update-slice_fusion.9
  139.9 1.4 bitcast_dynamic-update-slice_fusion.9
  141.4 8.5 %while.4 = (s32[]{:T(128)}, bf16[512,512]{1,0:T(8,128)(2,1)S(1)}, s32[4,2]{0,1:T(2,128)S(1)}, bf16[4,256,256]{2,1,0:T(8,128)(2,1)S(1)}, s32[]{:T(128)}) while((s32[]{:T(128)}, bf16[512,512]{1,0:T(8,128)(2,1)S(1)}, s32[4,2]{0,1:T(2,128)S(1)}, bf16[4,256,256]{2,1,0:T(8,128)(2,1)S(1)}, s32[]{:T(128)}) %tuple.125), condition=%wide.while_cond, body=%wide.while_body.sunk | while | flops 2 | bytes 262261 | solution.py:165
  142.1 1.4 bitcast_dynamic-update-slice_fusion.8
  144.2 1.4 bitcast_dynamic-update-slice_fusion.8
  146.4 1.4 bitcast_dynamic-update-slice_fusion.8
  148.5 1.4 bitcast_dynamic-update-slice_fusion.8
  149.9 1.1 slice_bitcast_fusion.2
  151.4 4.8 %add_convert_fusion.3 = (bf16[4,256,256]{1,2,0:T(8,128)(2,1)S(1)}, bf16[4,256,256]{1,2,0:T(8,128)(2,1)S(1)}) fusion(f32[256,256]{0,1:T(8,128)S(1)} %copy.657, s32[4,256]{1,0:T(4,128)S(1)} %get-tuple-element.150, s32[4,256]{1,0:T(4,128)S(1)} %get-tuple-element.151, f32[256,256]{0,1:T(8,128)S(1)} %copy.656), kind=kLoop, calls=%fused_computation.206 | loop fusion | flops 5767168 | bytes 1581056 | tf_op jit(solution)/shard_map/convert_element_type | solution.py:83
  156.2 0.7 convolution_bitcast_fusion.7
  157.2 0.8 fusion.77
  158.0 4.1 %fusion.30 = (bf16[4,256,256]{2,1,0:T(8,128)(2,1)S(1)}, bf16[4,256,256]{2,1,0:T(8,128)(2,1)S(1)}) fusion(bf16[4,256,256]{2,1,0:T(8,128)(2,1)S(1)} %get-tuple-element.12, f32[8,256,512]{2,1,0:T(8,128)S(1)} %fusion.77), kind=kLoop, calls=%fused_computation.63 | loop fusion | flops 2883584 | bytes 5767168 | tf_op jit(solution)/shard_map/convert_element_type | solution.py:56
  162.1 0.8 convolution_bitcast_fusion.6
  163.3 0.8 fusion.84
  164.1 4.7 %fusion.147 = (f32[256,256]{0,1:T(8,128)S(1)}, f32[256,256]{0,1:T(8,128)S(1)}, f32[256,256]{0,1:T(8,128)S(1)}, f32[256,256]{0,1:T(8,128)S(1)}, f32[256,256]{0,1:T(8,128)S(1)}, /*index=5*/f32[256,256]{0,1:T(8,128)S(1)}) fusion(f32[]{:T(128)} %bitcast.11, s32[256]{0:T(256)S(1)} %fusion.169, f32[]{:T(128)} %bitcast.17, f32[]{:T(128)} %bitcast.14), kind=kLoop, calls=%fused_computation.227 | loop fusion | flops 983040 | bytes 1573900 | tf_op jit(solution)/shard_map/mul | solution.py:96
  169.3 0.7 convolution_bitcast_fusion.5
  170.3 0.8 fusion.91
  171.1 4.3 %fusion.26 = (bf16[4,256,256]{2,1,0:T(8,128)(2,1)S(1)}, bf16[4,256,256]{2,1,0:T(8,128)(2,1)S(1)}) fusion(bf16[4,256,256]{2,1,0:T(8,128)(2,1)S(1)} %get-tuple-element.20, f32[8,256,512]{2,1,0:T(8,128)S(1)} %fusion.91), kind=kLoop, calls=%fused_computation.59 | loop fusion | flops 2883584 | bytes 5767168 | tf_op jit(solution)/shard_map/convert_element_type | solution.py:56
  175.4 0.8 convolution_bitcast_fusion.4
  176.6 0.8 fusion.98
  177.8 0.7 convolution_bitcast_fusion.3
  178.9 0.8 fusion.105
  179.6 4.1 %fusion.22 = (bf16[4,256,256]{2,1,0:T(8,128)(2,1)S(1)}, bf16[4,256,256]{2,1,0:T(8,128)(2,1)S(1)}) fusion(bf16[4,256,256]{2,1,0:T(8,128)(2,1)S(1)} %get-tuple-element.28, f32[8,256,512]{2,1,0:T(8,128)S(1)} %fusion.105), kind=kLoop, calls=%fused_computation.55 | loop fusion | flops 2883584 | bytes 5767168 | tf_op jit(solution)/shard_map/convert_element_type | solution.py:56
  183.8 0.8 convolution_bitcast_fusion.2
  184.9 0.8 fusion.112
  186.2 0.7 convolution_bitcast_fusion.1
  187.2 0.8 fusion.119
  188.0 4.4 %fusion.18 = (bf16[4,256,256]{2,1,0:T(8,128)(2,1)S(1)}, bf16[4,256,256]{2,1,0:T(8,128)(2,1)S(1)}) fusion(bf16[4,256,256]{2,1,0:T(8,128)(2,1)S(1)} %get-tuple-element.36, f32[8,256,512]{2,1,0:T(8,128)S(1)} %fusion.119), kind=kLoop, calls=%fused_computation.51 | loop fusion | flops 2883584 | bytes 5767168 | tf_op jit(solution)/shard_map/convert_element_type | solution.py:56
  192.4 0.8 convolution_bitcast_fusion
  193.5 0.8 fusion.126
  195.1 1.0 fusion.193
  196.1 0.7 constant_dynamic-update-slice_fusion.15
  196.8 0.7 constant_dynamic-update-slice_fusion.14
  197.5 0.7 constant_dynamic-update-slice_fusion.13
  198.1 0.7 constant_dynamic-update-slice_fusion.12
  198.8 0.7 constant_dynamic-update-slice_fusion.11
  199.4 0.7 constant_dynamic-update-slice_fusion.10
  201.4 0.7 constant_dynamic-update-slice_fusion.7
  203.4 0.7 constant_dynamic-update-slice_fusion.4
  205.4 0.7 constant_dynamic-update-slice_fusion.1
  206.7 6.8 %all-to-all-start = ((bf16[16,4,1,4096]{3,1,2,0:T(4,128)(2,1)}), bf16[16,4,1,4096]{3,1,2,0:T(4,128)(2,1)S(1)}, u32[]{:S(2)}, u32[]{:S(2)}) async-start(bf16[16,4,1,4096]{3,1,2,0:T(4,128)(2,1)} %constant_dynamic-update-slice_fusion), calls=%async_computation | async-start | bytes 1048576 | tf_op jit(solution)/shard_map/all_to_all | solution.py:15
  213.6 14.1 %all-to-all-done = bf16[16,4,1,4096]{3,1,2,0:T(4,128)(2,1)S(1)} async-done(((bf16[16,4,1,4096]{3,1,2,0:T(4,128)(2,1)}), bf16[16,4,1,4096]{3,1,2,0:T(4,128)(2,1)S(1)}, u32[]{:S(2)}, u32[]{:S(2)}) %all-to-all-start) | async-done | bytes 524320 | tf_op jit(solution)/shard_map/all_to_all | solution.py:15
  228.5 1.5 pad_maximum_fusion
  (78 shorter events, 22.5 us)
Async XLA Ops:
  9.5 98.2 %copy-start.1 = (s32[4,2]{0,1:T(2,128)S(1)}, s32[4,2]{0,1:T(2,128)}, u32[]{:S(2)}) copy-start(s32[4,2]{0,1:T(2,128)} %param.15) | copy-start | bytes 100
  106.6 13.2 %copy-start = (f32[3]{0:T(128)S(1)}, f32[3]{0:T(128)}, u32[]{:S(2)}) copy-start(f32[3]{0:T(128)} %param.17) | copy-start | bytes 40
  119.8 31.3 %copy-start.2 = (s32[4,2]{0,1:T(2,128)S(1)}, s32[4,2]{0,1:T(2,128)}, u32[]{:S(2)}) copy-start(s32[4,2]{0,1:T(2,128)} %param.16) | copy-start | bytes 100
  206.7 21.1 %all-to-all-start = ((bf16[16,4,1,4096]{3,1,2,0:T(4,128)(2,1)}), bf16[16,4,1,4096]{3,1,2,0:T(4,128)(2,1)S(1)}, u32[]{:S(2)}, u32[]{:S(2)}) async-start(bf16[16,4,1,4096]{3,1,2,0:T(4,128)(2,1)} %constant_dynamic-update-slice_fusion), calls=%async_computation | async-start | bytes 1048576 | tf_op jit(solution)/shard_map/all_to_all | solution.py:15
